TPU v7x, 32 devices: a whole 2x2x4 slice. The times are simulated.
32 devices in a mesh: group: 2 (over y), space: 4 (over x, core), src: 4 (over z).
Axes of the slice: x: 2, y: 2, z: 4, core: 2. Of those that a mesh axis runs over, the one named last changes fastest.
Arguments:
- conductivity: float32 [128, 32, 128], P(('group', 'space')), parts along dimension 0, may hold values from 0.2 to 5
- prior_potential: float32 [8, 64, 32, 128], P(('group', 'src'), 'space'), parts along dimension 0, may hold values from -6 to 6
- electrodes: int32 [8, 2], P(('group', 'src')), parts along dimension 0, may hold values from 0 to 262143
- currents: float32 [8], P(('group', 'src')), parts along dimension 0, may hold values from 2 to 20
- receivers: int32 [512], P('group'), parts along dimension 0, may hold values from 0 to 262143
- observed: float32 [8, 256], P(('group', 'src')), parts along dimension 0, may hold values from -3 to 3
Outputs:
- potential: float32 [8, 64, 32, 128], P(('group', 'src'), 'space'), parts along dimension 0
- misfit: float32 [8, 256], P(('group', 'src')), parts along dimension 0
- gradient: float32 [128, 32, 128], P(('group', 'space')), parts along dimension 0
There are 2 independent parts, one for each index of `group`. A program takes and returns all parts, laid end to end along the dimension named above; each array names one. Nothing has to cross between parts.
Inputs may be any that keep to these rules, and one draw needn't show every extreme that they name: Flat cell indices x * 32 * 128 + y * 128 + z; a source's two electrodes may fall in any cells. Flat cell indices as for electrodes; two receivers may share a cell.
All inputs are finite; a program needn't handle non-finite values.
Results may differ from a plain program's by a relative error of at most 0.0003.
Values sent between devices are 32-bit elements; how exact they have to be, the bound alone decides.
No kernel may reach another device: no remote copies, remote signals or barrier semaphores. Data moves between devices by JAX's collectives and lax.ppermute only.
A program may use at most 128 MiB of HBM per device.

v0:
```python
import jax
import jax.numpy as jnp
from jax import lax
from jax.sharding import PartitionSpec as P

LEVELS = 4
COARSE_SWEEPS = 4
OFFSETS = ((1, 0, 0), (-1, 0, 0), (0, 1, 0), (0, -1, 0), (0, 0, 1), (0, 0, -1))


def padded_2(block, sides, width):
    for axis, dim in sides:
        count = lax.axis_size(axis)
        forward = [(i, i + 1) for i in range(count - 1)]
        backward = [(target, source) for source, target in forward]
        low = lax.ppermute(
            lax.slice_in_dim(block, block.shape[dim] - width, None, axis=dim), axis, forward
        )
        high = lax.ppermute(lax.slice_in_dim(block, 0, width, axis=dim), axis, backward)
        block = jnp.concatenate([low, block, high], axis=dim)
    return block


def shifted(array, step):
    size_x, size_y, size_z = array.shape[-3:]
    return array[
        ...,
        1 + step[0] : size_x - 1 + step[0],
        1 + step[1] : size_y - 1 + step[1],
        1 + step[2] : size_z - 1 + step[2],
    ]


def couplings(sigma_ext, weight):
    padded = jnp.pad(sigma_ext, ((0, 0), (1, 1), (1, 1)))
    centre = shifted(padded, (0, 0, 0))
    return [weight * 0.5 * (centre + shifted(padded, step)) for step in OFFSETS]


def diagonal_of(coupled):
    summed = coupled[0]
    for coupling in coupled[1:]:
        summed = summed + coupling
    return summed


def neighbours(field_ext, coupled):
    padded = jnp.pad(field_ext, ((0, 0), (0, 0), (1, 1), (1, 1)))
    summed = coupled[0] * shifted(padded, OFFSETS[0])
    for coupling, step in zip(coupled[1:], OFFSETS[1:]):
        summed = summed + coupling * shifted(padded, step)
    return summed


def relax(field_ext, right_side, coupled, diagonal, colour_mask):
    update = (right_side + neighbours(field_ext, coupled)) / diagonal
    return jnp.where(colour_mask, update, field_ext[:, 1:-1])


def parity(planes, cells_y, cells_z, first_plane):
    plane_x = first_plane + lax.iota(jnp.int32, planes)
    plane_y = lax.iota(jnp.int32, cells_y)
    plane_z = lax.iota(jnp.int32, cells_z)
    summed = plane_x[:, None, None] + plane_y[None, :, None] + plane_z[None, None, :]
    return summed % 2 == 0


def boundary_planes(field_now, width):
    return padded_2(field_now, (("space", 1),), width)


def coarsen(array):
    size_x, size_y, size_z = array.shape[-3:]
    leading = array.shape[:-3]
    blocks = array.reshape(leading + (size_x // 2, 2, size_y // 2, 2, size_z // 2, 2))
    return blocks.mean(axis=(-5, -3, -1))


def refine(array):
    return jnp.repeat(jnp.repeat(jnp.repeat(array, 2, axis=-3), 2, axis=-2), 2, axis=-1)


def pairing(forward_ext, adjoint_ext):
    forward_mid = shifted(forward_ext, (0, 0, 0))
    adjoint_mid = shifted(adjoint_ext, (0, 0, 0))
    summed = jnp.zeros(forward_mid.shape, jnp.float32)
    for step in OFFSETS:
        summed = summed + (forward_mid - shifted(forward_ext, step)) * (
            adjoint_mid - shifted(adjoint_ext, step)
        )
    return -0.5 * jnp.sum(summed, axis=0)


def sweep_plain(field_now, right_side, grid_level, from_zero, extend):
    coupled, diagonal, red_mask = (grid_level[0], grid_level[1], grid_level[2])
    if from_zero:
        field_now = jnp.where(red_mask, right_side / diagonal, 0.0)
    else:
        field_now = relax(extend(field_now, 1), right_side, coupled, diagonal, red_mask)
    return relax(extend(field_now, 1), right_side, coupled, diagonal, jnp.logical_not(red_mask))


def smooth(field_now, right_side, grid_level, from_zero):
    return sweep_plain(field_now, right_side, grid_level, from_zero, boundary_planes)


def residual_of(field_now, right_side, grid_level):
    coupled, diagonal = (grid_level[0], grid_level[1])
    return right_side - (diagonal * field_now - neighbours(boundary_planes(field_now, 1), coupled))


def cycle(levels, level_index, right_side, field_now, from_zero):
    grid_level = levels[level_index]
    if level_index == len(levels) - 1:
        for sweep_index in range(COARSE_SWEEPS):
            field_now = smooth(field_now, right_side, grid_level, sweep_index == 0)
        return field_now
    field_now = smooth(field_now, right_side, grid_level, from_zero)
    coarse_rhs = coarsen(residual_of(field_now, right_side, grid_level))
    correction = cycle(levels, level_index + 1, coarse_rhs, None, True)
    field_now = field_now + refine(correction)
    return smooth(field_now, right_side, grid_level, False)


def body(conductivity, prior_potential, electrodes, currents, receivers, observed):
    rim_width = 1
    position = lax.axis_index("space")
    levels = []
    sigma_level = conductivity
    for level_index in range(LEVELS):
        planes, cells_y, cells_z = sigma_level.shape
        weight = 0.25**level_index
        extended = boundary_planes(sigma_level[None], rim_width)[0]
        coupled_all = couplings(extended, weight)
        red_mask = parity(planes, cells_y, cells_z, position * planes)
        levels.append((coupled_all, diagonal_of(coupled_all), red_mask, None, None, None))
        if level_index < LEVELS - 1:
            sigma_level = coarsen(sigma_level)
    sources, planes, cells_y, cells_z = prior_potential.shape
    cell_count = planes * cells_y * cells_z
    offset = position * cell_count

    def placed(flat_index):
        local_index = flat_index - offset
        return jnp.where((local_index >= 0) & (local_index < cell_count), local_index, cell_count)

    source_rows = jnp.arange(sources, dtype=jnp.int32)
    source = jnp.zeros((sources, cell_count), jnp.float32)
    source = source.at[source_rows, placed(electrodes[:, 0])].add(currents, mode="drop")
    source = source.at[source_rows, placed(electrodes[:, 1])].add(-currents, mode="drop")
    source = source.reshape(sources, planes, cells_y, cells_z)
    potential = cycle(levels, 0, source, prior_potential, False)
    local_index = receivers - offset
    inside_mask = (local_index >= 0) & (local_index < cell_count)
    picked = jnp.take(
        potential.reshape(sources, cell_count), jnp.clip(local_index, 0, cell_count - 1), axis=1
    )
    partial_values = jnp.where(inside_mask[None, :], picked, 0.0)
    at_receivers = lax.psum(partial_values, "space")
    misfit = at_receivers - observed
    adjoint_source = (
        jnp.zeros((sources, cell_count), jnp.float32)
        .at[:, placed(receivers)]
        .add(misfit, mode="drop")
    )
    adjoint = cycle(
        levels, 0, adjoint_source.reshape(sources, planes, cells_y, cells_z), None, True
    )
    stacked = boundary_planes(jnp.concatenate((potential, adjoint), 0), 1)
    stacked = jnp.pad(stacked, ((0, 0), (0, 0), (1, 1), (1, 1)))
    local_terms = pairing(stacked[:sources], stacked[sources:])
    gradient = lax.psum(local_terms, "src")
    return (potential, misfit, gradient)


def solution(mesh):
    return jax.shard_map(
        body,
        mesh=mesh,
        in_specs=(
            P(("group", "space"), None, None),
            P(("group", "src"), "space", None, None),
            P(("group", "src"), None),
            P(("group", "src")),
            P("group"),
            P(("group", "src"), None),
        ),
        out_specs=(
            P(("group", "src"), "space", None, None),
            P(("group", "src"), None),
            P(("group", "space"), None, None),
        ),
        check_vma=False,
    )
```

profile of v0, /device:TPU:0, one launch (start us, length us, event | category | flops | bytes accessed | tf_op | source)
XLA Modules:
  0.0 483.4 jit_solution(1726280062933962700)
XLA Ops:
  12.3 5.1 %collective-permute-start.3 = (f32[1,1,32,128]{3,2,1,0:T(8,128)S(1)}, f32[1,1,32,128]{3,2,1,0:T(8,128)S(1)}, u32[]{:S(2)}, u32[]{:S(2)}) collective-permute-start(f32[1,1,32,128]{3,2,1,0:T(8,128)S(1)} %get-tuple-element.78), channel_id=1, source_target_pairs={{0,4},{4,8},{8,12},{1,5},{5,9},{9,13},{2,6},{6,10},{10,14},{3,7},{... | collective-permute-start | bytes 49160 | tf_op jit(solution)/shard_map/ppermute | solution.py:16
  18.8 18.9 %reshape.630 = f32[8,2,16,2,64,2]{5,4,3,2,1,0:T(8,128)} reshape(f32[16,32,128]{2,1,0:T(8,128)} %param.10) | data formatting | bytes 524288 | tf_op jit(solution)/shard_map/reshape | solution.py:75
  37.6 7.0 %reduce_sum.86 = f32[8,16,64]{2,1,0:T(8,128)S(1)} reduce(f32[8,2,16,2,64,2]{5,4,3,2,1,0:T(8,128)} %reshape.630, f32[]{:T(128)} %constant.147.clone.1), dimensions={1,3,5}, to_apply=%region_3.4 | reduce | flops 57344 | bytes 294916 | tf_op jit(solution)/shard_map/reduce_sum | solution.py:76
  56.9 4.9 %collective-permute-start.9 = (f32[1,1,16,64]{3,2,1,0:T(8,128)S(1)}, f32[1,1,16,64]{3,2,1,0:T(8,128)S(1)}, u32[]{:S(2)}, u32[]{:S(2)}) collective-permute-start(f32[1,1,16,64]{3,2,1,0:T(8,128)S(1)} %get-tuple-element.99), channel_id=1, source_target_pairs={{0,4},{4,8},{8,12},{1,5},{5,9},{9,13},{2,6},{6,10},{10,14},{3,7},{... | collective-permute-start | bytes 12296 | tf_op jit(solution)/shard_map/ppermute | solution.py:16
  64.0 4.3 collective-permute-start.5
  69.7 4.3 collective-permute-start.15
  76.0 4.3 collective-permute-start.7
  85.3 18.1 %reshape.629 = f32[8,2,16,2,64,2]{5,4,3,2,1,0:T(8,128)} reshape(f32[1,16,32,128]{3,2,1,0:T(8,128)S(1)} %fusion.94) | data formatting | bytes 524288 | tf_op jit(solution)/shard_map/reshape | solution.py:75
  103.4 7.0 %reduce_sum.85 = f32[8,16,64]{2,1,0:T(8,128)S(1)} reduce(f32[8,2,16,2,64,2]{5,4,3,2,1,0:T(8,128)} %reshape.629, f32[]{:T(128)} %constant.147.clone.1), dimensions={1,3,5}, to_apply=%region_2.3 | reduce | flops 57344 | bytes 294916 | tf_op jit(solution)/shard_map/reduce_sum | solution.py:76
  110.6 4.4 collective-permute-start.11
  217.6 3.9 collective-permute-start.43
  229.2 3.8 collective-permute-start.45
  236.9 3.9 collective-permute-start.47
  246.5 7.7 %psum.14 = f32[1,256]{1,0:T(1,128)S(1)} all-reduce(f32[1,256]{1,0:T(1,128)S(1)} %bitcast.510), channel_id=1, replica_groups=mesh['group'=2,'space'=4,'src'=4] {'space'}, use_global_device_ids=true, to_apply=%region_8.9 | all-reduce | flops 256 | bytes 2048 | tf_op jit(solution)/shard_map/psum | solution.py:159
  263.4 4.4 collective-permute-start.51
  271.6 18.1 %reshape.636 = f32[8,2,16,2,64,2]{5,4,3,2,1,0:T(8,128)} reshape(f32[1,16,32,128]{3,2,1,0:T(8,128)S(1)} %fusion.55) | data formatting | bytes 524288 | tf_op jit(solution)/shard_map/reshape | solution.py:75
  289.7 7.0 %reduce_sum.91 = f32[8,16,64]{2,1,0:T(8,128)S(1)} reduce(f32[8,2,16,2,64,2]{5,4,3,2,1,0:T(8,128)} %reshape.636, f32[]{:T(128)} %constant.147.clone.1), dimensions={1,3,5}, to_apply=%region_10.11 | reduce | flops 57344 | bytes 294916 | tf_op jit(solution)/shard_map/reduce_sum | solution.py:76
  296.9 3.9 collective-permute-start.53
  316.8 3.8 collective-permute-start.57
  402.7 3.9 collective-permute-start.81
  413.1 3.8 collective-permute-start.83
  420.7 3.9 collective-permute-start.85
  428.5 3.9 collective-permute-start.87
  437.2 37.6 %all-reduce.46.cloned.1.call-done = f32[16,32,128]{2,1,0:T(8,128)} async-done(((f32[16,32,128]{2,1,0:T(8,128)}), f32[16,32,128]{2,1,0:T(8,128)}) %all-reduce.46.cloned.1.call-update) | async-done | bytes 262160 | tf_op jit(solution)/shard_map/psum | solution.py:172
  (469 shorter events, 274.1 us)
Async XLA Ops:
  7.2 467.7 %all-reduce.46.cloned.1.call-start = ((), (), s32[]{:S(2)}) async-start(), calls=%async_computation | async-start | bytes 524288 | tf_op jit(solution)/shard_map/psum | solution.py:172
  8.0 48.9 %collective-permute-start.2 = (f32[1,1,32,128]{3,2,1,0:T(8,128)S(1)}, f32[1,1,32,128]{3,2,1,0:T(8,128)S(1)}, u32[]{:S(2)}, u32[]{:S(2)}) collective-permute-start(f32[1,1,32,128]{3,2,1,0:T(8,128)S(1)} %get-tuple-element.76), channel_id=1, source_target_pairs={{0,4},{4,8},{8,12},{1,5},{5,9},{9,13},{2,6},{6,10},{10,14},{3,7},{... | collective-permute-start | bytes 49160 | tf_op jit(solution)/shard_map/ppermute | solution.py:16
  10.3 51.5 %collective-permute-start = (f32[1,1,32,128]{3,2,1,0:T(8,128)S(1)}, f32[1,1,32,128]{3,2,1,0:T(8,128)S(1)}, u32[]{:S(2)}, u32[]{:S(2)}) collective-permute-start(f32[1,1,32,128]{3,2,1,0:T(8,128)S(1)} %get-tuple-element.77), channel_id=1, source_target_pairs={{4,0},{8,4},{12,8},{5,1},{9,5},{13,9},{6,2},{10,6},{14,10},{7,3},{... | collective-permute-start | bytes 49160 | tf_op jit(solution)/shard_map/ppermute | solution.py:19
  12.3 50.8 %collective-permute-start.3 = (f32[1,1,32,128]{3,2,1,0:T(8,128)S(1)}, f32[1,1,32,128]{3,2,1,0:T(8,128)S(1)}, u32[]{:S(2)}, u32[]{:S(2)}) collective-permute-start(f32[1,1,32,128]{3,2,1,0:T(8,128)S(1)} %get-tuple-element.78), channel_id=1, source_target_pairs={{0,4},{4,8},{8,12},{1,5},{5,9},{9,13},{2,6},{6,10},{10,14},{3,7},{... | collective-permute-start | bytes 49160 | tf_op jit(solution)/shard_map/ppermute | solution.py:16
  17.5 45.6 %collective-permute-start.1 = (f32[1,1,32,128]{3,2,1,0:T(8,128)S(1)}, f32[1,1,32,128]{3,2,1,0:T(8,128)S(1)}, u32[]{:S(2)}, u32[]{:S(2)}) collective-permute-start(f32[1,1,32,128]{3,2,1,0:T(8,128)S(1)} %get-tuple-element.79), channel_id=1, source_target_pairs={{4,0},{8,4},{12,8},{5,1},{9,5},{13,9},{6,2},{10,6},{14,10},{7,3},{... | collective-permute-start | bytes 49160 | tf_op jit(solution)/shard_map/ppermute | solution.py:19
  44.7 31.3 %collective-permute-start.8 = (f32[1,1,16,64]{3,2,1,0:T(8,128)S(1)}, f32[1,1,16,64]{3,2,1,0:T(8,128)S(1)}, u32[]{:S(2)}, u32[]{:S(2)}) collective-permute-start(f32[1,1,16,64]{3,2,1,0:T(8,128)S(1)} %get-tuple-element.98), channel_id=1, source_target_pairs={{4,0},{8,4},{12,8},{5,1},{9,5},{13,9},{6,2},{10,6},{14,10},{7,3},{... | collective-permute-start | bytes 12296 | tf_op jit(solution)/shard_map/ppermute | solution.py:19
  56.9 23.5 %collective-permute-start.9 = (f32[1,1,16,64]{3,2,1,0:T(8,128)S(1)}, f32[1,1,16,64]{3,2,1,0:T(8,128)S(1)}, u32[]{:S(2)}, u32[]{:S(2)}) collective-permute-start(f32[1,1,16,64]{3,2,1,0:T(8,128)S(1)} %get-tuple-element.99), channel_id=1, source_target_pairs={{0,4},{4,8},{8,12},{1,5},{5,9},{9,13},{2,6},{6,10},{10,14},{3,7},{... | collective-permute-start | bytes 12296 | tf_op jit(solution)/shard_map/ppermute | solution.py:16
  61.8 61.1 %collective-permute-start.14 = (f32[1,1,8,32]{3,2,1,0:T(8,128)}, f32[1,1,8,32]{3,2,1,0:T(8,128)S(1)}, u32[]{:S(2)}, u32[]{:S(2)}) collective-permute-start(f32[1,1,8,32]{3,2,1,0:T(8,128)} %get-tuple-element.118), channel_id=1, source_target_pairs={{4,0},{8,4},{12,8},{5,1},{9,5},{13,9},{6,2},{10,6},{14,10},{7,3},{... | collective-permute-start | bytes 3080 | tf_op jit(solution)/shard_map/ppermute | solution.py:19
  64.0 5.7 %collective-permute-start.5 = (f32[1,1,32,128]{3,2,1,0:T(8,128)S(1)}, f32[1,1,32,128]{3,2,1,0:T(8,128)S(1)}, u32[]{:S(2)}, u32[]{:S(2)}) collective-permute-start(f32[1,1,32,128]{3,2,1,0:T(8,128)S(1)} %get-tuple-element.74), channel_id=1, source_target_pairs={{0,4},{4,8},{8,12},{1,5},{5,9},{9,13},{2,6},{6,10},{10,14},{3,7},{... | collective-permute-start | bytes 49160 | tf_op jit(solution)/shard_map/ppermute | solution.py:16
  68.3 5.6 %collective-permute-start.4 = (f32[1,1,32,128]{3,2,1,0:T(8,128)S(1)}, f32[1,1,32,128]{3,2,1,0:T(8,128)S(1)}, u32[]{:S(2)}, u32[]{:S(2)}) collective-permute-start(f32[1,1,32,128]{3,2,1,0:T(8,128)S(1)} %get-tuple-element.75), channel_id=1, source_target_pairs={{4,0},{8,4},{12,8},{5,1},{9,5},{13,9},{6,2},{10,6},{14,10},{7,3},{... | collective-permute-start | bytes 49160 | tf_op jit(solution)/shard_map/ppermute | solution.py:19
  69.7 54.7 %collective-permute-start.15 = (f32[1,1,8,32]{3,2,1,0:T(8,128)}, f32[1,1,8,32]{3,2,1,0:T(8,128)S(1)}, u32[]{:S(2)}, u32[]{:S(2)}) collective-permute-start(f32[1,1,8,32]{3,2,1,0:T(8,128)} %get-tuple-element.119), channel_id=1, source_target_pairs={{0,4},{4,8},{8,12},{1,5},{5,9},{9,13},{2,6},{6,10},{10,14},{3,7},{... | collective-permute-start | bytes 3080 | tf_op jit(solution)/shard_map/ppermute | solution.py:16
  74.0 69.9 %collective-permute-start.20 = (f32[1,1,4,16]{3,2,1,0:T(4,128)}, f32[1,1,4,16]{3,2,1,0:T(4,128)S(1)}, u32[]{:S(2)}, u32[]{:S(2)}) collective-permute-start(f32[1,1,4,16]{3,2,1,0:T(4,128)} %get-tuple-element.148), channel_id=1, source_target_pairs={{4,0},{8,4},{12,8},{5,1},{9,5},{13,9},{6,2},{10,6},{14,10},{7,3},{... | collective-permute-start | bytes 776 | tf_op jit(solution)/shard_map/ppermute | solution.py:19
  76.0 5.6 %collective-permute-start.7 = (f32[1,1,32,128]{3,2,1,0:T(8,128)S(1)}, f32[1,1,32,128]{3,2,1,0:T(8,128)S(1)}, u32[]{:S(2)}, u32[]{:S(2)}) collective-permute-start(f32[1,1,32,128]{3,2,1,0:T(8,128)S(1)} %get-tuple-element.72), channel_id=1, source_target_pairs={{0,4},{4,8},{8,12},{1,5},{5,9},{9,13},{2,6},{6,10},{10,14},{3,7},{... | collective-permute-start | bytes 49160 | tf_op jit(solution)/shard_map/ppermute | solution.py:16
  110.6 5.7 %collective-permute-start.11 = (f32[1,1,16,64]{3,2,1,0:T(8,128)S(1)}, f32[1,1,16,64]{3,2,1,0:T(8,128)S(1)}, u32[]{:S(2)}, u32[]{:S(2)}) collective-permute-start(f32[1,1,16,64]{3,2,1,0:T(8,128)S(1)} %get-tuple-element.96), channel_id=1, source_target_pairs={{0,4},{4,8},{8,12},{1,5},{5,9},{9,13},{2,6},{6,10},{10,14},{3,7},{... | collective-permute-start | bytes 12296 | tf_op jit(solution)/shard_map/ppermute | solution.py:16
  116.3 27.5 %collective-permute-start.21 = (f32[1,1,4,16]{3,2,1,0:T(4,128)S(1)}, f32[1,1,4,16]{3,2,1,0:T(4,128)S(1)}, u32[]{:S(2)}, u32[]{:S(2)}) collective-permute-start(f32[1,1,4,16]{3,2,1,0:T(4,128)S(1)} %copy-done.45), channel_id=1, source_target_pairs={{0,4},{4,8},{8,12},{1,5},{5,9},{9,13},{2,6},{6,10},{10,14},{3,7},{... | collective-permute-start | bytes 776 | tf_op jit(solution)/shard_map/ppermute | solution.py:16
  131.6 5.2 %collective-permute-start.17 = (f32[1,1,8,32]{3,2,1,0:T(8,128)S(1)}, f32[1,1,8,32]{3,2,1,0:T(8,128)S(1)}, u32[]{:S(2)}, u32[]{:S(2)}) collective-permute-start(f32[1,1,8,32]{3,2,1,0:T(8,128)S(1)} %get-tuple-element.116), channel_id=1, source_target_pairs={{0,4},{4,8},{8,12},{1,5},{5,9},{9,13},{2,6},{6,10},{10,14},{3,7},{... | collective-permute-start | bytes 3080 | tf_op jit(solution)/shard_map/ppermute | solution.py:16
  217.6 5.2 %collective-permute-start.43 = (f32[1,1,16,64]{3,2,1,0:T(8,128)S(1)}, f32[1,1,16,64]{3,2,1,0:T(8,128)S(1)}, u32[]{:S(2)}, u32[]{:S(2)}) collective-permute-start(f32[1,1,16,64]{3,2,1,0:T(8,128)S(1)} %get-tuple-element.88), channel_id=1, source_target_pairs={{0,4},{4,8},{8,12},{1,5},{5,9},{9,13},{2,6},{6,10},{10,14},{3,7},{... | collective-permute-start | bytes 12296 | tf_op jit(solution)/shard_map/ppermute | solution.py:16
  229.2 5.8 %collective-permute-start.45 = (f32[1,1,32,128]{3,2,1,0:T(8,128)S(1)}, f32[1,1,32,128]{3,2,1,0:T(8,128)S(1)}, u32[]{:S(2)}, u32[]{:S(2)}) collective-permute-start(f32[1,1,32,128]{3,2,1,0:T(8,128)S(1)} %get-tuple-element.70), channel_id=1, source_target_pairs={{0,4},{4,8},{8,12},{1,5},{5,9},{9,13},{2,6},{6,10},{10,14},{3,7},{... | collective-permute-start | bytes 49160 | tf_op jit(solution)/shard_map/ppermute | solution.py:16
  236.9 5.2 %collective-permute-start.47 = (f32[1,1,32,128]{3,2,1,0:T(8,128)S(1)}, f32[1,1,32,128]{3,2,1,0:T(8,128)S(1)}, u32[]{:S(2)}, u32[]{:S(2)}) collective-permute-start(f32[1,1,32,128]{3,2,1,0:T(8,128)S(1)} %get-tuple-element.68), channel_id=1, source_target_pairs={{0,4},{4,8},{8,12},{1,5},{5,9},{9,13},{2,6},{6,10},{10,14},{3,7},{... | collective-permute-start | bytes 49160 | tf_op jit(solution)/shard_map/ppermute | solution.py:16
  263.4 5.9 %collective-permute-start.51 = (f32[1,1,32,128]{3,2,1,0:T(8,128)S(1)}, f32[1,1,32,128]{3,2,1,0:T(8,128)S(1)}, u32[]{:S(2)}, u32[]{:S(2)}) collective-permute-start(f32[1,1,32,128]{3,2,1,0:T(8,128)S(1)} %get-tuple-element.64), channel_id=1, source_target_pairs={{0,4},{4,8},{8,12},{1,5},{5,9},{9,13},{2,6},{6,10},{10,14},{3,7},{... | collective-permute-start | bytes 49160 | tf_op jit(solution)/shard_map/ppermute | solution.py:16
  296.9 5.2 %collective-permute-start.53 = (f32[1,1,16,64]{3,2,1,0:T(8,128)S(1)}, f32[1,1,16,64]{3,2,1,0:T(8,128)S(1)}, u32[]{:S(2)}, u32[]{:S(2)}) collective-permute-start(f32[1,1,16,64]{3,2,1,0:T(8,128)S(1)} %get-tuple-element.86), channel_id=1, source_target_pairs={{0,4},{4,8},{8,12},{1,5},{5,9},{9,13},{2,6},{6,10},{10,14},{3,7},{... | collective-permute-start | bytes 12296 | tf_op jit(solution)/shard_map/ppermute | solution.py:16
  402.7 5.2 %collective-permute-start.81 = (f32[1,1,16,64]{3,2,1,0:T(8,128)S(1)}, f32[1,1,16,64]{3,2,1,0:T(8,128)S(1)}, u32[]{:S(2)}, u32[]{:S(2)}) collective-permute-start(f32[1,1,16,64]{3,2,1,0:T(8,128)S(1)} %get-tuple-element.80), channel_id=1, source_target_pairs={{0,4},{4,8},{8,12},{1,5},{5,9},{9,13},{2,6},{6,10},{10,14},{3,7},{... | collective-permute-start | bytes 12296 | tf_op jit(solution)/shard_map/ppermute | solution.py:16
  420.7 5.2 %collective-permute-start.85 = (f32[1,1,32,128]{3,2,1,0:T(8,128)S(1)}, f32[1,1,32,128]{3,2,1,0:T(8,128)S(1)}, u32[]{:S(2)}, u32[]{:S(2)}) collective-permute-start(f32[1,1,32,128]{3,2,1,0:T(8,128)S(1)} %get-tuple-element.60), channel_id=1, source_target_pairs={{0,4},{4,8},{8,12},{1,5},{5,9},{9,13},{2,6},{6,10},{10,14},{3,7},{... | collective-permute-start | bytes 49160 | tf_op jit(solution)/shard_map/ppermute | solution.py:16
  428.5 5.2 %collective-permute-start.87 = (f32[2,1,32,128]{3,2,1,0:T(8,128)S(1)}, f32[2,1,32,128]{3,2,1,0:T(8,128)S(1)}, u32[]{:S(2)}, u32[]{:S(2)}) collective-permute-start(f32[2,1,32,128]{3,2,1,0:T(8,128)S(1)} %get-tuple-element.58), channel_id=1, source_target_pairs={{0,4},{4,8},{8,12},{1,5},{5,9},{9,13},{2,6},{6,10},{10,14},{3,7},{... | collective-permute-start | bytes 98312 | tf_op jit(solution)/shard_map/ppermute | solution.py:16
  (113 other events, 2511.1 us)
Sparse Core Ops, SparseCore 0:
  437.4 37.4 all-reduce.45
where the time goes:
time: 486 us; the launch traced here: 483 us
  starting transfers between devices  225 us (46%)
  waiting for transfers between devices  104 us (21%)
  local copies, waits for them, and re-layouts  79.4 us (16%)
  other arithmetic  45.4 us (9%)
  between operations  21.3 us (4%)
  blocking collectives  7.67 us (2%)
    ppermute x44, starting transfers between devices, padded_2(): lax.ppermute(lax.slice_in_dim(block, block.shape[dim] - width, None, axis...  168 us
    ppermute x44, waiting for transfers between devices, padded_2(): lax.ppermute(lax.slice_in_dim(block, 0, width, axis=dim), axis, backward)  66.6 us
    reshape x7, local copies, waits for them, and re-layouts, coarsen(): array.reshape(leading + (size_x // 2, 2, size_y // 2, 2, size_z // 2, 2))  62.3 us
    ppermute x44, starting transfers between devices, padded_2(): lax.ppermute(lax.slice_in_dim(block, 0, width, axis=dim), axis, backward)  57.3 us
    psum x1, waiting for transfers between devices, body(): gradient = lax.psum(local_terms, 'src')  37.6 us
    reduce_sum x9, other arithmetic, coarsen(): return blocks.mean(axis=(-5, -3, -1))  25.2 us
  transfers between devices with their start and end apart: 89, of which 38 were waited for; matrix products, arithmetic and copies ran while one was open for 14% of the time, Pallas kernels for 0%

commit v1 on v0

--- a/solution.py
+++ b/solution.py
@@ -169,7 +169,9 @@
     stacked = boundary_planes(jnp.concatenate((potential, adjoint), 0), 1)
     stacked = jnp.pad(stacked, ((0, 0), (0, 0), (1, 1), (1, 1)))
     local_terms = pairing(stacked[:sources], stacked[sources:])
-    gradient = lax.psum(local_terms, "src")
+    gradient = local_terms
+    for hop in (1, 2):
+        gradient = gradient + lax.ppermute(gradient, "src", [(dev, dev ^ hop) for dev in range(4)])
     return (potential, misfit, gradient)
 
 

time: 486 us -> 457 us (0.940)
  waiting for transfers between devices: 104 us -> 86.1 us
  between operations: 21.3 us -> 7.94 us
    psum x1 -> x0, waiting for transfers between devices: 37.6 us -> none  [body(): gradient = lax.psum(local_terms, 'src')]
    ppermute x0 -> x2, waiting for transfers between devices: none -> 19.4 us  [body(): lax.ppermute(gradient, 'src', [(dev, dev ^ hop) for dev in range(4)])]
  transfers between devices with their start and end apart: 89 -> 90, of which waited for: 38 -> 39; matrix products, arithmetic and copies ran while one was open for 14% -> 15% of each run, Pallas kernels for 0% -> 0%
where the time goes in v1:
time: 457 us; the launch traced here: 454 us
  starting transfers between devices  229 us (50%)
  waiting for transfers between devices  86.1 us (19%)
  local copies, waits for them, and re-layouts  77.7 us (17%)
  other arithmetic  45.5 us (10%)
  between operations  7.94 us (2%)
  blocking collectives  7.67 us (2%)
    ppermute x44, starting transfers between devices, padded_2(): lax.ppermute(lax.slice_in_dim(block, block.shape[dim] - width, None, axis...  168 us
    ppermute x44, waiting for transfers between devices, padded_2(): lax.ppermute(lax.slice_in_dim(block, 0, width, axis=dim), axis, backward)  66.6 us
    reshape x7, local copies, waits for them, and re-layouts, coarsen(): array.reshape(leading + (size_x // 2, 2, size_y // 2, 2, size_z // 2, 2))  62.3 us
    ppermute x44, starting transfers between devices, padded_2(): lax.ppermute(lax.slice_in_dim(block, 0, width, axis=dim), axis, backward)  57.3 us
    reduce_sum x9, other arithmetic, coarsen(): return blocks.mean(axis=(-5, -3, -1))  25.2 us
    ppermute x2, waiting for transfers between devices, body(): lax.ppermute(gradient, 'src', [(dev, dev ^ hop) for dev in range(4)])  19.4 us
  transfers between devices with their start and end apart: 90, of which 39 were waited for; matrix products, arithmetic and copies ran while one was open for 15% of the time, Pallas kernels for 0%

profile of v1, /device:TPU:0, one launch (start us, length us, event | category | flops | bytes accessed | tf_op | source)
XLA Modules:
  0.0 454.4 jit_solution(1584425331305118795)
XLA Ops:
  5.8 5.1 %collective-permute-start.3 = (f32[1,1,32,128]{3,2,1,0:T(8,128)S(1)}, f32[1,1,32,128]{3,2,1,0:T(8,128)S(1)}, u32[]{:S(2)}, u32[]{:S(2)}) collective-permute-start(f32[1,1,32,128]{3,2,1,0:T(8,128)S(1)} %get-tuple-element.78), channel_id=1, source_target_pairs={{0,4},{4,8},{8,12},{1,5},{5,9},{9,13},{2,6},{6,10},{10,14},{3,7},{... | collective-permute-start | bytes 49160 | tf_op jit(solution)/shard_map/ppermute | solution.py:16
  12.2 18.9 %reshape.630 = f32[8,2,16,2,64,2]{5,4,3,2,1,0:T(8,128)} reshape(f32[16,32,128]{2,1,0:T(8,128)} %param.10) | data formatting | bytes 524288 | tf_op jit(solution)/shard_map/reshape | solution.py:75
  31.1 7.0 %reduce_sum.86 = f32[8,16,64]{2,1,0:T(8,128)S(1)} reduce(f32[8,2,16,2,64,2]{5,4,3,2,1,0:T(8,128)} %reshape.630, f32[]{:T(128)} %constant.147.clone.1), dimensions={1,3,5}, to_apply=%region_3.4 | reduce | flops 57344 | bytes 294916 | tf_op jit(solution)/shard_map/reduce_sum | solution.py:76
  50.3 4.9 %collective-permute-start.9 = (f32[1,1,16,64]{3,2,1,0:T(8,128)S(1)}, f32[1,1,16,64]{3,2,1,0:T(8,128)S(1)}, u32[]{:S(2)}, u32[]{:S(2)}) collective-permute-start(f32[1,1,16,64]{3,2,1,0:T(8,128)S(1)} %get-tuple-element.99), channel_id=1, source_target_pairs={{0,4},{4,8},{8,12},{1,5},{5,9},{9,13},{2,6},{6,10},{10,14},{3,7},{... | collective-permute-start | bytes 12296 | tf_op jit(solution)/shard_map/ppermute | solution.py:16
  57.5 4.3 collective-permute-start.5
  63.1 4.3 collective-permute-start.15
  69.5 4.3 collective-permute-start.7
  78.8 18.1 %reshape.629 = f32[8,2,16,2,64,2]{5,4,3,2,1,0:T(8,128)} reshape(f32[1,16,32,128]{3,2,1,0:T(8,128)S(1)} %fusion.94) | data formatting | bytes 524288 | tf_op jit(solution)/shard_map/reshape | solution.py:75
  96.9 7.0 %reduce_sum.85 = f32[8,16,64]{2,1,0:T(8,128)S(1)} reduce(f32[8,2,16,2,64,2]{5,4,3,2,1,0:T(8,128)} %reshape.629, f32[]{:T(128)} %constant.147.clone.1), dimensions={1,3,5}, to_apply=%region_2.3 | reduce | flops 57344 | bytes 294916 | tf_op jit(solution)/shard_map/reduce_sum | solution.py:76
  104.0 4.4 collective-permute-start.11
  211.0 3.9 collective-permute-start.43
  222.7 3.8 collective-permute-start.45
  230.4 3.9 collective-permute-start.47
  239.9 7.7 %psum.7 = f32[1,256]{1,0:T(1,128)S(1)} all-reduce(f32[1,256]{1,0:T(1,128)S(1)} %bitcast.510), channel_id=1, replica_groups=mesh['group'=2,'space'=4,'src'=4] {'space'}, use_global_device_ids=true, to_apply=%region_8.9 | all-reduce | flops 256 | bytes 2048 | tf_op jit(solution)/shard_map/psum | solution.py:159
  256.9 4.4 collective-permute-start.51
  265.0 18.1 %reshape.636 = f32[8,2,16,2,64,2]{5,4,3,2,1,0:T(8,128)} reshape(f32[1,16,32,128]{3,2,1,0:T(8,128)S(1)} %fusion.55) | data formatting | bytes 524288 | tf_op jit(solution)/shard_map/reshape | solution.py:75
  283.1 7.0 %reduce_sum.91 = f32[8,16,64]{2,1,0:T(8,128)S(1)} reduce(f32[8,2,16,2,64,2]{5,4,3,2,1,0:T(8,128)} %reshape.636, f32[]{:T(128)} %constant.147.clone.1), dimensions={1,3,5}, to_apply=%region_10.11 | reduce | flops 57344 | bytes 294916 | tf_op jit(solution)/shard_map/reduce_sum | solution.py:76
  290.3 3.9 collective-permute-start.53
  396.1 3.9 collective-permute-start.81
  406.5 3.8 collective-permute-start.83
  414.2 3.9 collective-permute-start.85
  421.9 3.9 collective-permute-start.87
  431.6 6.4 %collective-permute-done.88 = f32[16,32,128]{2,1,0:T(8,128)S(1)} collective-permute-done((f32[16,32,128]{2,1,0:T(8,128)S(1)}, f32[16,32,128]{2,1,0:T(8,128)S(1)}, u32[]{:S(2)}, u32[]{:S(2)}) %collective-permute-start.88) | collective-permute-done | bytes 262176 | tf_op jit(solution)/shard_map/ppermute | solution.py:174
  440.7 13.0 %collective-permute-done.89 = f32[16,32,128]{2,1,0:T(8,128)S(1)} collective-permute-done((f32[16,32,128]{2,1,0:T(8,128)S(1)}, f32[16,32,128]{2,1,0:T(8,128)S(1)}, u32[]{:S(2)}, u32[]{:S(2)}) %collective-permute-start.89) | collective-permute-done | bytes 262176 | tf_op jit(solution)/shard_map/ppermute | solution.py:174
  (471 shorter events, 280.6 us)
Async XLA Ops:
  1.4 48.9 %collective-permute-start.2 = (f32[1,1,32,128]{3,2,1,0:T(8,128)S(1)}, f32[1,1,32,128]{3,2,1,0:T(8,128)S(1)}, u32[]{:S(2)}, u32[]{:S(2)}) collective-permute-start(f32[1,1,32,128]{3,2,1,0:T(8,128)S(1)} %get-tuple-element.76), channel_id=1, source_target_pairs={{0,4},{4,8},{8,12},{1,5},{5,9},{9,13},{2,6},{6,10},{10,14},{3,7},{... | collective-permute-start | bytes 49160 | tf_op jit(solution)/shard_map/ppermute | solution.py:16
  3.7 51.5 %collective-permute-start = (f32[1,1,32,128]{3,2,1,0:T(8,128)S(1)}, f32[1,1,32,128]{3,2,1,0:T(8,128)S(1)}, u32[]{:S(2)}, u32[]{:S(2)}) collective-permute-start(f32[1,1,32,128]{3,2,1,0:T(8,128)S(1)} %get-tuple-element.77), channel_id=1, source_target_pairs={{4,0},{8,4},{12,8},{5,1},{9,5},{13,9},{6,2},{10,6},{14,10},{7,3},{... | collective-permute-start | bytes 49160 | tf_op jit(solution)/shard_map/ppermute | solution.py:19
  5.8 50.8 %collective-permute-start.3 = (f32[1,1,32,128]{3,2,1,0:T(8,128)S(1)}, f32[1,1,32,128]{3,2,1,0:T(8,128)S(1)}, u32[]{:S(2)}, u32[]{:S(2)}) collective-permute-start(f32[1,1,32,128]{3,2,1,0:T(8,128)S(1)} %get-tuple-element.78), channel_id=1, source_target_pairs={{0,4},{4,8},{8,12},{1,5},{5,9},{9,13},{2,6},{6,10},{10,14},{3,7},{... | collective-permute-start | bytes 49160 | tf_op jit(solution)/shard_map/ppermute | solution.py:16
  10.9 45.7 %collective-permute-start.1 = (f32[1,1,32,128]{3,2,1,0:T(8,128)S(1)}, f32[1,1,32,128]{3,2,1,0:T(8,128)S(1)}, u32[]{:S(2)}, u32[]{:S(2)}) collective-permute-start(f32[1,1,32,128]{3,2,1,0:T(8,128)S(1)} %get-tuple-element.79), channel_id=1, source_target_pairs={{4,0},{8,4},{12,8},{5,1},{9,5},{13,9},{6,2},{10,6},{14,10},{7,3},{... | collective-permute-start | bytes 49160 | tf_op jit(solution)/shard_map/ppermute | solution.py:19
  38.1 31.4 %collective-permute-start.8 = (f32[1,1,16,64]{3,2,1,0:T(8,128)S(1)}, f32[1,1,16,64]{3,2,1,0:T(8,128)S(1)}, u32[]{:S(2)}, u32[]{:S(2)}) collective-permute-start(f32[1,1,16,64]{3,2,1,0:T(8,128)S(1)} %get-tuple-element.98), channel_id=1, source_target_pairs={{4,0},{8,4},{12,8},{5,1},{9,5},{13,9},{6,2},{10,6},{14,10},{7,3},{... | collective-permute-start | bytes 12296 | tf_op jit(solution)/shard_map/ppermute | solution.py:19
  50.3 23.5 %collective-permute-start.9 = (f32[1,1,16,64]{3,2,1,0:T(8,128)S(1)}, f32[1,1,16,64]{3,2,1,0:T(8,128)S(1)}, u32[]{:S(2)}, u32[]{:S(2)}) collective-permute-start(f32[1,1,16,64]{3,2,1,0:T(8,128)S(1)} %get-tuple-element.99), channel_id=1, source_target_pairs={{0,4},{4,8},{8,12},{1,5},{5,9},{9,13},{2,6},{6,10},{10,14},{3,7},{... | collective-permute-start | bytes 12296 | tf_op jit(solution)/shard_map/ppermute | solution.py:16
  55.2 61.1 %collective-permute-start.14 = (f32[1,1,8,32]{3,2,1,0:T(8,128)}, f32[1,1,8,32]{3,2,1,0:T(8,128)S(1)}, u32[]{:S(2)}, u32[]{:S(2)}) collective-permute-start(f32[1,1,8,32]{3,2,1,0:T(8,128)} %get-tuple-element.118), channel_id=1, source_target_pairs={{4,0},{8,4},{12,8},{5,1},{9,5},{13,9},{6,2},{10,6},{14,10},{7,3},{... | collective-permute-start | bytes 3080 | tf_op jit(solution)/shard_map/ppermute | solution.py:19
  57.5 5.7 %collective-permute-start.5 = (f32[1,1,32,128]{3,2,1,0:T(8,128)S(1)}, f32[1,1,32,128]{3,2,1,0:T(8,128)S(1)}, u32[]{:S(2)}, u32[]{:S(2)}) collective-permute-start(f32[1,1,32,128]{3,2,1,0:T(8,128)S(1)} %get-tuple-element.74), channel_id=1, source_target_pairs={{0,4},{4,8},{8,12},{1,5},{5,9},{9,13},{2,6},{6,10},{10,14},{3,7},{... | collective-permute-start | bytes 49160 | tf_op jit(solution)/shard_map/ppermute | solution.py:16
  61.7 5.6 %collective-permute-start.4 = (f32[1,1,32,128]{3,2,1,0:T(8,128)S(1)}, f32[1,1,32,128]{3,2,1,0:T(8,128)S(1)}, u32[]{:S(2)}, u32[]{:S(2)}) collective-permute-start(f32[1,1,32,128]{3,2,1,0:T(8,128)S(1)} %get-tuple-element.75), channel_id=1, source_target_pairs={{4,0},{8,4},{12,8},{5,1},{9,5},{13,9},{6,2},{10,6},{14,10},{7,3},{... | collective-permute-start | bytes 49160 | tf_op jit(solution)/shard_map/ppermute | solution.py:19
  63.1 54.6 %collective-permute-start.15 = (f32[1,1,8,32]{3,2,1,0:T(8,128)}, f32[1,1,8,32]{3,2,1,0:T(8,128)S(1)}, u32[]{:S(2)}, u32[]{:S(2)}) collective-permute-start(f32[1,1,8,32]{3,2,1,0:T(8,128)} %get-tuple-element.119), channel_id=1, source_target_pairs={{0,4},{4,8},{8,12},{1,5},{5,9},{9,13},{2,6},{6,10},{10,14},{3,7},{... | collective-permute-start | bytes 3080 | tf_op jit(solution)/shard_map/ppermute | solution.py:16
  67.4 69.8 %collective-permute-start.20 = (f32[1,1,4,16]{3,2,1,0:T(4,128)}, f32[1,1,4,16]{3,2,1,0:T(4,128)S(1)}, u32[]{:S(2)}, u32[]{:S(2)}) collective-permute-start(f32[1,1,4,16]{3,2,1,0:T(4,128)} %get-tuple-element.148), channel_id=1, source_target_pairs={{4,0},{8,4},{12,8},{5,1},{9,5},{13,9},{6,2},{10,6},{14,10},{7,3},{... | collective-permute-start | bytes 776 | tf_op jit(solution)/shard_map/ppermute | solution.py:19
  69.5 5.6 %collective-permute-start.7 = (f32[1,1,32,128]{3,2,1,0:T(8,128)S(1)}, f32[1,1,32,128]{3,2,1,0:T(8,128)S(1)}, u32[]{:S(2)}, u32[]{:S(2)}) collective-permute-start(f32[1,1,32,128]{3,2,1,0:T(8,128)S(1)} %get-tuple-element.72), channel_id=1, source_target_pairs={{0,4},{4,8},{8,12},{1,5},{5,9},{9,13},{2,6},{6,10},{10,14},{3,7},{... | collective-permute-start | bytes 49160 | tf_op jit(solution)/shard_map/ppermute | solution.py:16
  104.0 5.7 %collective-permute-start.11 = (f32[1,1,16,64]{3,2,1,0:T(8,128)S(1)}, f32[1,1,16,64]{3,2,1,0:T(8,128)S(1)}, u32[]{:S(2)}, u32[]{:S(2)}) collective-permute-start(f32[1,1,16,64]{3,2,1,0:T(8,128)S(1)} %get-tuple-element.96), channel_id=1, source_target_pairs={{0,4},{4,8},{8,12},{1,5},{5,9},{9,13},{2,6},{6,10},{10,14},{3,7},{... | collective-permute-start | bytes 12296 | tf_op jit(solution)/shard_map/ppermute | solution.py:16
  109.8 27.5 %collective-permute-start.21 = (f32[1,1,4,16]{3,2,1,0:T(4,128)S(1)}, f32[1,1,4,16]{3,2,1,0:T(4,128)S(1)}, u32[]{:S(2)}, u32[]{:S(2)}) collective-permute-start(f32[1,1,4,16]{3,2,1,0:T(4,128)S(1)} %copy-done.45), channel_id=1, source_target_pairs={{0,4},{4,8},{8,12},{1,5},{5,9},{9,13},{2,6},{6,10},{10,14},{3,7},{... | collective-permute-start | bytes 776 | tf_op jit(solution)/shard_map/ppermute | solution.py:16
  125.0 5.2 %collective-permute-start.17 = (f32[1,1,8,32]{3,2,1,0:T(8,128)S(1)}, f32[1,1,8,32]{3,2,1,0:T(8,128)S(1)}, u32[]{:S(2)}, u32[]{:S(2)}) collective-permute-start(f32[1,1,8,32]{3,2,1,0:T(8,128)S(1)} %get-tuple-element.116), channel_id=1, source_target_pairs={{0,4},{4,8},{8,12},{1,5},{5,9},{9,13},{2,6},{6,10},{10,14},{3,7},{... | collective-permute-start | bytes 3080 | tf_op jit(solution)/shard_map/ppermute | solution.py:16
  222.7 5.8 %collective-permute-start.45 = (f32[1,1,32,128]{3,2,1,0:T(8,128)S(1)}, f32[1,1,32,128]{3,2,1,0:T(8,128)S(1)}, u32[]{:S(2)}, u32[]{:S(2)}) collective-permute-start(f32[1,1,32,128]{3,2,1,0:T(8,128)S(1)} %get-tuple-element.70), channel_id=1, source_target_pairs={{0,4},{4,8},{8,12},{1,5},{5,9},{9,13},{2,6},{6,10},{10,14},{3,7},{... | collective-permute-start | bytes 49160 | tf_op jit(solution)/shard_map/ppermute | solution.py:16
  230.4 5.2 %collective-permute-start.47 = (f32[1,1,32,128]{3,2,1,0:T(8,128)S(1)}, f32[1,1,32,128]{3,2,1,0:T(8,128)S(1)}, u32[]{:S(2)}, u32[]{:S(2)}) collective-permute-start(f32[1,1,32,128]{3,2,1,0:T(8,128)S(1)} %get-tuple-element.68), channel_id=1, source_target_pairs={{0,4},{4,8},{8,12},{1,5},{5,9},{9,13},{2,6},{6,10},{10,14},{3,7},{... | collective-permute-start | bytes 49160 | tf_op jit(solution)/shard_map/ppermute | solution.py:16
  256.9 5.9 %collective-permute-start.51 = (f32[1,1,32,128]{3,2,1,0:T(8,128)S(1)}, f32[1,1,32,128]{3,2,1,0:T(8,128)S(1)}, u32[]{:S(2)}, u32[]{:S(2)}) collective-permute-start(f32[1,1,32,128]{3,2,1,0:T(8,128)S(1)} %get-tuple-element.64), channel_id=1, source_target_pairs={{0,4},{4,8},{8,12},{1,5},{5,9},{9,13},{2,6},{6,10},{10,14},{3,7},{... | collective-permute-start | bytes 49160 | tf_op jit(solution)/shard_map/ppermute | solution.py:16
  290.3 5.2 %collective-permute-start.53 = (f32[1,1,16,64]{3,2,1,0:T(8,128)S(1)}, f32[1,1,16,64]{3,2,1,0:T(8,128)S(1)}, u32[]{:S(2)}, u32[]{:S(2)}) collective-permute-start(f32[1,1,16,64]{3,2,1,0:T(8,128)S(1)} %get-tuple-element.86), channel_id=1, source_target_pairs={{0,4},{4,8},{8,12},{1,5},{5,9},{9,13},{2,6},{6,10},{10,14},{3,7},{... | collective-permute-start | bytes 12296 | tf_op jit(solution)/shard_map/ppermute | solution.py:16
  396.1 5.2 %collective-permute-start.81 = (f32[1,1,16,64]{3,2,1,0:T(8,128)S(1)}, f32[1,1,16,64]{3,2,1,0:T(8,128)S(1)}, u32[]{:S(2)}, u32[]{:S(2)}) collective-permute-start(f32[1,1,16,64]{3,2,1,0:T(8,128)S(1)} %get-tuple-element.80), channel_id=1, source_target_pairs={{0,4},{4,8},{8,12},{1,5},{5,9},{9,13},{2,6},{6,10},{10,14},{3,7},{... | collective-permute-start | bytes 12296 | tf_op jit(solution)/shard_map/ppermute | solution.py:16
  414.2 5.2 %collective-permute-start.85 = (f32[1,1,32,128]{3,2,1,0:T(8,128)S(1)}, f32[1,1,32,128]{3,2,1,0:T(8,128)S(1)}, u32[]{:S(2)}, u32[]{:S(2)}) collective-permute-start(f32[1,1,32,128]{3,2,1,0:T(8,128)S(1)} %get-tuple-element.60), channel_id=1, source_target_pairs={{0,4},{4,8},{8,12},{1,5},{5,9},{9,13},{2,6},{6,10},{10,14},{3,7},{... | collective-permute-start | bytes 49160 | tf_op jit(solution)/shard_map/ppermute | solution.py:16
  421.9 5.2 %collective-permute-start.87 = (f32[2,1,32,128]{3,2,1,0:T(8,128)S(1)}, f32[2,1,32,128]{3,2,1,0:T(8,128)S(1)}, u32[]{:S(2)}, u32[]{:S(2)}) collective-permute-start(f32[2,1,32,128]{3,2,1,0:T(8,128)S(1)} %get-tuple-element.58), channel_id=1, source_target_pairs={{0,4},{4,8},{8,12},{1,5},{5,9},{9,13},{2,6},{6,10},{10,14},{3,7},{... | collective-permute-start | bytes 98312 | tf_op jit(solution)/shard_map/ppermute | solution.py:16
  429.9 8.0 %collective-permute-start.88 = (f32[16,32,128]{2,1,0:T(8,128)S(1)}, f32[16,32,128]{2,1,0:T(8,128)S(1)}, u32[]{:S(2)}, u32[]{:S(2)}) collective-permute-start(f32[16,32,128]{2,1,0:T(8,128)S(1)} %fusion.21), channel_id=1, source_target_pairs={{0,1},{1,0},{2,3},{3,2},{4,5},{5,4},{6,7},{7,6},{8,9},{9,8},{10,11... | collective-permute-start | bytes 786440 | tf_op jit(solution)/shard_map/ppermute | solution.py:174
  438.0 15.7 %collective-permute-start.89 = (f32[16,32,128]{2,1,0:T(8,128)S(1)}, f32[16,32,128]{2,1,0:T(8,128)S(1)}, u32[]{:S(2)}, u32[]{:S(2)}) collective-permute-start(f32[16,32,128]{2,1,0:T(8,128)S(1)} %add.1628), channel_id=1, source_target_pairs={{0,2},{1,3},{2,0},{3,1},{4,6},{5,7},{6,4},{7,5},{8,10},{9,11},{10,... | collective-permute-start | bytes 786440 | tf_op jit(solution)/shard_map/ppermute | solution.py:174
  (114 other events, 2516.3 us)
